TPU v7x, 32 devices: a whole 2x2x4 slice. The times are simulated.
32 devices in a mesh: section: 2 (over y), dp: 16 (over z, x, core).
Axes of the slice: x: 2, y: 2, z: 4, core: 2. Of those that a mesh axis runs over, the one named last changes fastest.
Arguments:
- tokens: bfloat16 [2, 4096, 768], P(None, 'dp'), may hold values from -6 to 6
- lengths: int32 [2, 16], replicated, may hold values from 200 to 256
- w_qkv: float32 [2, 768, 2304], P('section', 'dp'), may hold values from -0.21875 to 0.21875
- w_out: float32 [2, 768, 768], P('section', 'dp'), may hold values from -0.625 to 0.625
- w_gate_up: float32 [2, 768, 6144], P('section', 'dp'), may hold values from -0.21875 to 0.21875
- w_down: float32 [2, 3072, 768], P('section', 'dp'), may hold values from -0.109375 to 0.109375
- norm_gain: float32 [2, 2, 768], P('section', None, 'dp'), may hold values from 0.25 to 1.75
- norm_bias: float32 [2, 2, 768], P('section', None, 'dp'), may hold values from -3 to 3
- cotangent: bfloat16 [2, 4096, 768], P(None, 'dp'), may hold values from -6 to 6
Outputs:
- layer_outputs: bfloat16 [2, 2, 4096, 768], P('section', None, 'dp')
- input_grads: float32 [2, 2, 4096, 768], P('section', None, 'dp')
- grad_w_qkv: float32 [2, 768, 2304], P('section', 'dp')
- grad_w_out: float32 [2, 768, 768], P('section', 'dp')
- grad_w_gate_up: float32 [2, 768, 6144], P('section', 'dp')
- grad_w_down: float32 [2, 3072, 768], P('section', 'dp')
- grad_norm_gain: float32 [2, 2, 768], P('section', None, 'dp')
- grad_norm_bias: float32 [2, 2, 768], P('section', None, 'dp')
Inputs may be any that keep to these rules, and one draw needn't show every extreme that they name: `lengths`: positions of a window from its length on are padding.
All inputs are finite; a program needn't handle non-finite values.
Results may differ from a plain program's by a relative error of at most 0.024.
The roundings to bfloat16 on the way count: a program that leaves them out, or rounds other values in their place, can miss the bound.
Values may be sent and summed in bfloat16 or wider, within the bound.
No kernel may reach another device: no remote copies, remote signals or barrier semaphores. Data moves between devices by JAX's collectives and lax.ppermute only.
A program may use at most 256 MiB of HBM per device.

v0:
```python
import jax
import jax.numpy as jnp
from jax import lax
from jax.sharding import PartitionSpec as P

D = 768
HEADS = 12
HEAD = 64
FF = 3072
EPSILON = 1e-05
NEGATIVE = -1e30


def shifted(shard, axis, by):
    devices = lax.axis_size(axis)
    pairs = [(i, i + by) for i in range(devices) if 0 <= i + by < devices]
    return lax.ppermute(shard, axis, pairs)


def norm_forward(row_values, gain_row, bias_row):
    center = row_values - jnp.mean(row_values, axis=-1, keepdims=True)
    scale_inv = lax.rsqrt(jnp.mean(center * center, axis=-1, keepdims=True) + EPSILON)
    normed = center * scale_inv
    return (normed * gain_row + bias_row, normed, scale_inv)


def norm_backward(upstream, normed, scale_inv, gain_row):
    scaled = upstream * gain_row
    inner_sum = (
        scaled
        - jnp.mean(scaled, axis=-1, keepdims=True)
        - normed * jnp.mean(scaled * normed, axis=-1, keepdims=True)
    )
    return (scale_inv * inner_sum, jnp.sum(upstream * normed, axis=0), jnp.sum(upstream, axis=0))


def score_block(queries, keys_all, length):
    seq_rows = queries.shape[0]
    slopes = jnp.exp2(-8.0 * (jnp.arange(HEADS).astype(jnp.float32) + 1.0) / HEADS)
    raw_scores = jnp.einsum(
        "qhd,khd->hqk", queries, keys_all, preferred_element_type=jnp.float32
    ) * HEAD ** (-0.5)
    places = jnp.arange(seq_rows, dtype=jnp.int32)
    distance = jnp.abs(places[:, None] - places[None, :]).astype(jnp.float32)
    raw_scores = raw_scores - slopes[:, None, None] * distance[None]
    key_valid = places < length
    return jnp.where(key_valid[None, None, :], raw_scores, NEGATIVE)


def layer_forward(inputs, length, weights):
    qkv_matrix, out_matrix, gate_matrix, down_matrix, gain_rows, bias_rows = weights
    seq_rows = inputs.shape[0]
    projected = jnp.dot(inputs, qkv_matrix, preferred_element_type=jnp.float32).astype(jnp.bfloat16)
    queries = projected[:, :D]
    key_values = projected[:, D:]
    scores = score_block(
        queries.reshape(seq_rows, HEADS, HEAD),
        key_values[:, :D].reshape(seq_rows, HEADS, HEAD),
        length,
    )
    row_peak = jnp.max(scores, axis=-1, keepdims=True)
    row_exp = jnp.exp(scores - row_peak)
    totals = jnp.sum(row_exp, axis=-1, keepdims=True)
    attn_probs = row_exp / totals
    log_sum = row_peak + jnp.log(totals)
    context = jnp.einsum(
        "hqk,khd->qhd",
        attn_probs.astype(jnp.bfloat16),
        key_values[:, D:].reshape(seq_rows, HEADS, HEAD),
        preferred_element_type=jnp.float32,
    )
    context = context.reshape(seq_rows, D).astype(jnp.bfloat16)
    attended = jnp.dot(context, out_matrix, preferred_element_type=jnp.float32)
    gain_float = gain_rows.astype(jnp.float32)
    bias_float = bias_rows.astype(jnp.float32)
    first_norm, normed_one, inv_one = norm_forward(
        inputs.astype(jnp.float32) + attended, gain_float[0], bias_float[0]
    )
    first_low = first_norm.astype(jnp.bfloat16)
    gate_up = jnp.dot(first_low, gate_matrix, preferred_element_type=jnp.float32)
    gated_rows = (jax.nn.gelu(gate_up[:, :FF], approximate=False) * gate_up[:, FF:]).astype(
        jnp.bfloat16
    )
    down_rows = jnp.dot(gated_rows, down_matrix, preferred_element_type=jnp.float32)
    layer_out, normed_two, inv_two = norm_forward(
        first_norm + down_rows, gain_float[1], bias_float[1]
    )
    stored = (
        inputs,
        queries,
        key_values,
        log_sum,
        context,
        normed_one,
        inv_one,
        first_low,
        gate_up,
        normed_two,
        inv_two,
    )
    return (layer_out, stored)


def layer_backward(upstream, stored, length, weights):
    qkv_matrix, out_matrix, gate_matrix, down_matrix, gain_rows, bias_rows = weights
    (
        inputs,
        queries,
        key_values,
        log_sum,
        context,
        normed_one,
        inv_one,
        first_low,
        gate_up,
        normed_two,
        inv_two,
    ) = stored
    seq_rows = inputs.shape[0]
    gain_float = gain_rows.astype(jnp.float32)
    grad_two, gain_two, bias_two = norm_backward(upstream, normed_two, inv_two, gain_float[1])
    down_grad = grad_two.astype(jnp.bfloat16)
    gate_vals = gate_up[:, :FF]
    up_vals = gate_up[:, FF:]
    gelu_vals = jax.nn.gelu(gate_vals, approximate=False)
    gated_rows = (gelu_vals * up_vals).astype(jnp.bfloat16)
    grad_down_w = jnp.einsum("tf,td->fd", gated_rows, down_grad, preferred_element_type=jnp.float32)
    grad_gated = jnp.einsum("td,fd->tf", down_grad, down_matrix, preferred_element_type=jnp.float32)
    gauss_cdf = 0.5 * (1.0 + lax.erf(gate_vals * 2.0 ** (-0.5)))
    density = jnp.exp(-0.5 * gate_vals * gate_vals) * (2.0 * jnp.pi) ** (-0.5)
    grad_gate = grad_gated * up_vals * (gauss_cdf + gate_vals * density)
    grad_up = grad_gated * gelu_vals
    gate_up_grad = jnp.concatenate([grad_gate, grad_up], axis=1).astype(jnp.bfloat16)
    grad_gu_w = jnp.einsum("td,tf->df", first_low, gate_up_grad, preferred_element_type=jnp.float32)
    grad_first = grad_two + jnp.einsum(
        "tf,df->td", gate_up_grad, gate_matrix, preferred_element_type=jnp.float32
    )
    grad_one, gain_one, bias_one = norm_backward(grad_first, normed_one, inv_one, gain_float[0])
    attn_grad = grad_one.astype(jnp.bfloat16)
    grad_out_w = jnp.einsum("td,te->de", context, attn_grad, preferred_element_type=jnp.float32)
    context_grad = jnp.einsum(
        "te,de->td", attn_grad, out_matrix, preferred_element_type=jnp.float32
    )
    context_grad = context_grad.astype(jnp.bfloat16).reshape(seq_rows, HEADS, HEAD)
    query_heads = queries.reshape(seq_rows, HEADS, HEAD)
    keys_all = key_values[:, :D].reshape(seq_rows, HEADS, HEAD)
    values_all = key_values[:, D:].reshape(seq_rows, HEADS, HEAD)
    scores = score_block(query_heads, keys_all, length)
    attn_probs = jnp.exp(scores - log_sum)
    prob_grad = jnp.einsum(
        "qhd,khd->hqk", context_grad, values_all, preferred_element_type=jnp.float32
    )
    inner_sum = jnp.sum(attn_probs * prob_grad, axis=-1, keepdims=True)
    score_grad = (attn_probs * (prob_grad - inner_sum)).astype(jnp.bfloat16)
    query_grad = jnp.einsum(
        "hqk,khd->qhd", score_grad, keys_all, preferred_element_type=jnp.float32
    ) * HEAD ** (-0.5)
    key_grad = jnp.einsum(
        "hqk,qhd->khd", score_grad, query_heads, preferred_element_type=jnp.float32
    ) * HEAD ** (-0.5)
    value_grad = jnp.einsum(
        "hqk,qhd->khd",
        attn_probs.astype(jnp.bfloat16),
        context_grad,
        preferred_element_type=jnp.float32,
    )
    qkv_grad = jnp.concatenate(
        [
            query_grad.reshape(seq_rows, D),
            key_grad.reshape(seq_rows, D),
            value_grad.reshape(seq_rows, D),
        ],
        axis=1,
    ).astype(jnp.bfloat16)
    grad_qkv_w = jnp.einsum("td,te->de", inputs, qkv_grad, preferred_element_type=jnp.float32)
    input_grad = grad_one + jnp.einsum(
        "te,de->td", qkv_grad, qkv_matrix, preferred_element_type=jnp.float32
    )
    grad_terms = (
        grad_qkv_w,
        grad_out_w,
        grad_gu_w,
        grad_down_w,
        jnp.stack([gain_one, gain_two]),
        jnp.stack([bias_one, bias_two]),
    )
    return (input_grad, grad_terms)


def store_slot(slot_index, active, buffer, new_value):
    previous = lax.dynamic_index_in_dim(buffer, slot_index, 0, keepdims=False)
    return lax.dynamic_update_index_in_dim(
        buffer, jnp.where(active, new_value, previous), slot_index, 0
    )


def shards(tokens, lengths, w_qkv, w_out, w_gate_up, w_down, norm_gain, norm_bias, cotangent):
    section_index = lax.axis_index("section")
    window = lax.axis_index("dp")
    micro_count = tokens.shape[0]
    seq_rows = tokens.shape[1]
    forward_weights = (
        lax.all_gather(w_qkv[0].astype(jnp.bfloat16), "dp", axis=0, tiled=True),
        lax.all_gather(w_out[0].astype(jnp.bfloat16), "dp", axis=0, tiled=True),
        lax.all_gather(w_gate_up[0].astype(jnp.bfloat16), "dp", axis=0, tiled=True),
        lax.all_gather(w_down[0].astype(jnp.bfloat16), "dp", axis=0, tiled=True),
        lax.all_gather(norm_gain[0].astype(jnp.bfloat16), "dp", axis=1, tiled=True),
        lax.all_gather(norm_bias[0].astype(jnp.bfloat16), "dp", axis=1, tiled=True),
    )

    def length_of(slot_index):
        length_row = lax.dynamic_index_in_dim(lengths, slot_index, 0, keepdims=False)
        return lax.dynamic_index_in_dim(length_row, window, 0, keepdims=False)

    def slot_zeros(shape, dtype):
        return jnp.zeros((micro_count,) + shape, dtype)

    stash_init = (
        slot_zeros((seq_rows, D), jnp.bfloat16),
        slot_zeros((seq_rows, D), jnp.bfloat16),
        slot_zeros((seq_rows, 2 * D), jnp.bfloat16),
        slot_zeros((HEADS, seq_rows, 1), jnp.float32),
        slot_zeros((seq_rows, D), jnp.bfloat16),
        slot_zeros((seq_rows, D), jnp.float32),
        slot_zeros((seq_rows, 1), jnp.float32),
        slot_zeros((seq_rows, D), jnp.bfloat16),
        slot_zeros((seq_rows, 2 * FF), jnp.float32),
        slot_zeros((seq_rows, D), jnp.float32),
        slot_zeros((seq_rows, 1), jnp.float32),
        slot_zeros((seq_rows, D), jnp.bfloat16),
    )

    def forward_tick(carry, tick_now):
        arrived, stash = carry
        offset = tick_now - section_index
        slot_index = jnp.clip(offset, 0, micro_count - 1)
        active = (offset >= 0) & (offset < micro_count)
        own_input = lax.dynamic_index_in_dim(tokens, slot_index, 0, keepdims=False)
        layer_input = jnp.where(section_index == 0, own_input, arrived)
        layer_out, stored = layer_forward(layer_input, length_of(slot_index), forward_weights)
        sent_rows = layer_out.astype(jnp.bfloat16)
        passed = shifted(sent_rows, "section", 1)
        stash = tuple(
            (
                store_slot(slot_index, active, buffer, new_value)
                for buffer, new_value in zip(stash, stored + (sent_rows,))
            )
        )
        return ((passed, stash), None)

    tick_list = jnp.arange(micro_count + 1, dtype=jnp.int32)
    start_rows = jnp.zeros((seq_rows, D), jnp.bfloat16)
    (unused, stash), unused_out = lax.scan(forward_tick, (start_rows, stash_init), tick_list)
    backward_weights = (
        lax.all_gather(w_qkv[0].astype(jnp.bfloat16), "dp", axis=0, tiled=True),
        lax.all_gather(w_out[0].astype(jnp.bfloat16), "dp", axis=0, tiled=True),
        lax.all_gather(w_gate_up[0].astype(jnp.bfloat16), "dp", axis=0, tiled=True),
        lax.all_gather(w_down[0].astype(jnp.bfloat16), "dp", axis=0, tiled=True),
        lax.all_gather(norm_gain[0].astype(jnp.bfloat16), "dp", axis=1, tiled=True),
        lax.all_gather(norm_bias[0].astype(jnp.bfloat16), "dp", axis=1, tiled=True),
    )

    def backward_tick(carry, tick_now):
        arrived, summed, grads_in = carry
        offset = tick_now - 1 + section_index
        slot_index = jnp.clip(offset, 0, micro_count - 1)
        active = (offset >= 0) & (offset < micro_count)
        cot_rows = lax.dynamic_index_in_dim(cotangent, slot_index, 0, keepdims=False).astype(
            jnp.float32
        )
        upstream = jnp.where(section_index == 1, cot_rows, arrived.astype(jnp.float32))
        stored = tuple(
            (
                lax.dynamic_index_in_dim(buffer, slot_index, 0, keepdims=False)
                for buffer in stash[:-1]
            )
        )
        input_grad, grad_terms = layer_backward(
            upstream, stored, length_of(slot_index), backward_weights
        )
        weight_flag = active.astype(jnp.float32)
        masked = tuple((term * weight_flag for term in grad_terms))
        summed = tuple((left + right for left, right in zip(summed, masked)))
        passed = shifted(input_grad.astype(jnp.bfloat16), "section", -1)
        grads_in = store_slot(slot_index, active, grads_in, input_grad)
        return ((passed, summed, grads_in), None)

    summed_init = (
        jnp.zeros((D, 3 * D), jnp.float32),
        jnp.zeros((D, D), jnp.float32),
        jnp.zeros((D, 2 * FF), jnp.float32),
        jnp.zeros((FF, D), jnp.float32),
        jnp.zeros((2, D), jnp.float32),
        jnp.zeros((2, D), jnp.float32),
    )
    grads_init = jnp.zeros((micro_count, seq_rows, D), jnp.float32)
    (unused_back, summed, grads_in), unused_list = lax.scan(
        backward_tick, (start_rows, summed_init, grads_init), tick_list
    )
    attn_share = (
        lax.psum_scatter(summed[0], "dp", scatter_dimension=0, tiled=True),
        lax.psum_scatter(summed[1], "dp", scatter_dimension=0, tiled=True),
        lax.psum_scatter(summed[4], "dp", scatter_dimension=1, tiled=True),
        lax.psum_scatter(summed[5], "dp", scatter_dimension=1, tiled=True),
    )
    gate_share = lax.psum_scatter(summed[2], "dp", scatter_dimension=0, tiled=True)
    down_share = lax.psum_scatter(summed[3], "dp", scatter_dimension=0, tiled=True)
    shares = (attn_share[0], attn_share[1], gate_share, down_share, attn_share[2], attn_share[3])
    return (
        stash[-1][None],
        grads_in[None],
        shares[0][None],
        shares[1][None],
        shares[2][None],
        shares[3][None],
        shares[4][None],
        shares[5][None],
    )


def solution(mesh):
    return jax.shard_map(
        shards,
        mesh=mesh,
        in_specs=(
            P(None, "dp", None),
            P(),
            P("section", "dp", None),
            P("section", "dp", None),
            P("section", "dp", None),
            P("section", "dp", None),
            P("section", None, "dp"),
            P("section", None, "dp"),
            P(None, "dp", None),
        ),
        out_specs=(
            P("section", None, "dp", None),
            P("section", None, "dp", None),
            P("section", "dp", None),
            P("section", "dp", None),
            P("section", "dp", None),
            P("section", "dp", None),
            P("section", None, "dp"),
            P("section", None, "dp"),
        ),
        check_vma=False,
    )
```

profile of v0, /device:TPU:0, one launch (start us, length us, event | category | flops | bytes accessed | tf_op | source)
XLA Modules:
  0.0 1286.7 jit_solution(15711562108209963430)
XLA Ops:
  13.9 24.4 %all-gather.2 = bf16[1,2,768]{1,0,2:T(2,128)(2,1)S(1)} all-gather(bf16[1,2,48]{1,0,2:T(2,128)(2,1)S(1)} %copy.83), channel_id=4, replica_groups=mesh['section'=2,'dp'=16] {'dp'}, dimensions={2}, use_global_device_ids=true | all-gather | bytes 3264 | tf_op jit(solution)/shard_map/all_gather | solution.py:207
  39.1 18.7 %all-gather.3 = bf16[1,2,768]{1,0,2:T(2,128)(2,1)S(1)} all-gather(bf16[1,2,48]{1,0,2:T(2,128)(2,1)S(1)} %copy.85), channel_id=5, replica_groups=mesh['section'=2,'dp'=16] {'dp'}, dimensions={2}, use_global_device_ids=true | all-gather | bytes 3264 | tf_op jit(solution)/shard_map/all_gather | solution.py:208
  58.7 42.9 %all-gather.11.cloned.1.call-done = bf16[1,768,2304]{2,1,0:T(8,128)(2,1)} async-done(((bf16[1,48,2304]{2,1,0:T(8,128)(2,1)}), bf16[1,768,2304]{2,1,0:T(8,128)(2,1)}) %all-gather.11.cloned.1.call-update) | async-done | bytes 3538960 | tf_op jit(solution)/shard_map/all_gather | solution.py:203
  101.6 55.1 %all-gather.17.cloned.1.call-done = bf16[1,3072,768]{2,1,0:T(8,128)(2,1)} async-done(((bf16[1,192,768]{2,1,0:T(8,128)(2,1)}), bf16[1,3072,768]{2,1,0:T(8,128)(2,1)}) %all-gather.17.cloned.1.call-update) | async-done | bytes 4718608 | tf_op jit(solution)/shard_map/all_gather | solution.py:206
  156.7 82.7 %all-gather.15.cloned.1.call-done = bf16[1,768,6144]{2,1,0:T(8,128)(2,1)} async-done(((bf16[1,48,6144]{2,1,0:T(8,128)(2,1)}), bf16[1,768,6144]{2,1,0:T(8,128)(2,1)}) %all-gather.15.cloned.1.call-update) | async-done | bytes 9437200 | tf_op jit(solution)/shard_map/all_gather | solution.py:205
  251.1 6.1 broadcast_in_dim.183
  257.3 182.2 %while.65 = (s32[]{:T(128)}, bf16[256,768]{1,0:T(8,128)(2,1)}, bf16[2,256,768]{2,1,0:T(8,128)(2,1)}, bf16[2,256,768]{2,1,0:T(8,128)(2,1)}, bf16[2,256,1536]{2,1,...) while((s32[]{:T(128)}, bf16[256,768]{1,0:T(8,128)(2,1)}, ...), condition=%wide.region_7.8_spmd, body=%wide.region_0.7_spmd.sunk | while | flops 5104144384 | bytes 246386960 | solution.py:253
  279.3 9.0 bitcast_dynamic-update-slice_fusion.15
  288.3 15.4 %fusion.202 = (f32[256]{0:T(256)S(1)}, f32[256,768]{1,0:T(8,128)S(1)}) fusion(bf16[3072,768]{1,0:T(8,128)(2,1)} %get-tuple-element.1968, f32[256,6144]{1,0:T(8,128)} %get-tuple-element.1817, f32[768]{0:T(1024)S(1)} %get-tuple-element.1814, f32[768]{0:T(1024)S(1)} %get-tuple-element.1815, f32[256]{0:T(256)S(1)} %add_rsqrt_fusion.4, ...), kind=kOutput, calls=%fused_computation.222.clone.1 | convolution fusion | flops 1261043456 | bytes 12592128 | tf_op jit(solution)/shard_map/while/body/eval_jaxpr/dot_general | solution.py:84
  339.9 9.0 bitcast_dynamic-update-slice_fusion.15
  348.9 15.3 %fusion.202 = (f32[256]{0:T(256)S(1)}, f32[256,768]{1,0:T(8,128)S(1)}) fusion(bf16[3072,768]{1,0:T(8,128)(2,1)} %get-tuple-element.1968, f32[256,6144]{1,0:T(8,128)} %get-tuple-element.1817, f32[768]{0:T(1024)S(1)} %get-tuple-element.1814, f32[768]{0:T(1024)S(1)} %get-tuple-element.1815, f32[256]{0:T(256)S(1)} %add_rsqrt_fusion.4, ...), kind=kOutput, calls=%fused_computation.222.clone.1 | convolution fusion | flops 1261043456 | bytes 12592128 | tf_op jit(solution)/shard_map/while/body/eval_jaxpr/dot_general | solution.py:84
  365.7 5.4 collective-permute-start
  400.7 9.0 bitcast_dynamic-update-slice_fusion.15
  409.8 15.4 %fusion.202 = (f32[256]{0:T(256)S(1)}, f32[256,768]{1,0:T(8,128)S(1)}) fusion(bf16[3072,768]{1,0:T(8,128)(2,1)} %get-tuple-element.1968, f32[256,6144]{1,0:T(8,128)} %get-tuple-element.1817, f32[768]{0:T(1024)S(1)} %get-tuple-element.1814, f32[768]{0:T(1024)S(1)} %get-tuple-element.1815, f32[256]{0:T(256)S(1)} %add_rsqrt_fusion.4, ...), kind=kOutput, calls=%fused_computation.222.clone.1 | convolution fusion | flops 1261043456 | bytes 12592128 | tf_op jit(solution)/shard_map/while/body/eval_jaxpr/dot_general | solution.py:84
  442.0 244.6 %while.66 = (s32[]{:T(128)}, bf16[256,768]{1,0:T(8,128)(2,1)}, f32[768,2304]{1,0:T(8,128)}, f32[768,768]{1,0:T(8,128)}, f32[768,6144]{1,0:T(8,128)}, /*index=5*/...) while((s32[]{:T(128)}, bf16[256,768]{1,0:T(8,128)(2,1)}, ...), condition=%wide.region_18.19_spmd.clone, body=%wide.region_8.18_spmd.clone.sunk | while | flops 10294599680 | bytes 342882656 | solution.py:297
  465.1 10.6 multiply_convert_fusion.8
  493.2 7.3 select_add_fusion.11
  505.6 8.4 select_add_fusion.10
  539.1 10.6 multiply_convert_fusion.8
  568.3 10.0 select_add_fusion.11
  578.3 7.2 select_add_fusion.8
  585.6 12.1 select_add_fusion.10
  624.4 10.6 multiply_convert_fusion.8
  653.6 10.0 select_add_fusion.11
  663.6 7.2 select_add_fusion.8
  670.9 12.1 select_add_fusion.10
  692.8 52.8 %reduce-scatter.21.cloned.1.call-done = f32[48,2]{1,0:T(8,128)} async-done(((f32[768,2]{1,0:T(8,128)}), f32[48,2]{1,0:T(8,128)}) %reduce-scatter.21.cloned.1.call-update) | async-done | bytes 400
  747.0 57.0 %reduce-scatter.19.cloned.1.call-done = f32[48,2]{1,0:T(8,128)} async-done(((f32[768,2]{1,0:T(8,128)}), f32[48,2]{1,0:T(8,128)}) %reduce-scatter.19.cloned.1.call-update) | async-done | bytes 400
  805.4 65.0 %reduce-scatter.13.cloned.1.call-done = f32[48,768]{1,0:T(8,128)} async-done(((f32[768,768]{1,0:T(8,128)}), f32[48,768]{1,0:T(8,128)}) %reduce-scatter.13.cloned.1.call-update) | async-done | bytes 147472 | tf_op jit(solution)/shard_map/reduce_scatter | solution.py:302
  870.4 94.1 %reduce-scatter.11.cloned.1.call-done = f32[48,2304]{1,0:T(8,128)} async-done(((f32[768,2304]{1,0:T(8,128)}), f32[48,2304]{1,0:T(8,128)}) %reduce-scatter.11.cloned.1.call-update) | async-done | bytes 442384 | tf_op jit(solution)/shard_map/reduce_scatter | solution.py:301
  964.5 115.6 %reduce-scatter.17.cloned.1.call-done = f32[192,768]{1,0:T(8,128)} async-done(((f32[3072,768]{1,0:T(8,128)}), f32[192,768]{1,0:T(8,128)}) %reduce-scatter.17.cloned.1.call-update) | async-done | bytes 589840 | tf_op jit(solution)/shard_map/reduce_scatter | solution.py:307
  1080.2 199.7 %reduce-scatter.15.cloned.1.call-done = f32[48,6144]{1,0:T(8,128)} async-done(((f32[768,6144]{1,0:T(8,128)}), f32[48,6144]{1,0:T(8,128)}) %reduce-scatter.15.cloned.1.call-update) | async-done | bytes 1179664 | tf_op jit(solution)/shard_map/reduce_scatter | solution.py:306
  (710 shorter events, 266.8 us)
Async XLA Ops:
  7.2 51.5 %all-gather.13.cloned.1.call-start = ((), (), s32[]{:S(2)}) async-start(), calls=%async_computation.11 | async-start | bytes 1253376 | tf_op jit(solution)/shard_map/all_gather | solution.py:204
  8.9 92.7 %all-gather.11.cloned.1.call-start = ((), (), s32[]{:S(2)}) async-start(), calls=%async_computation.10 | async-start | bytes 3760128 | tf_op jit(solution)/shard_map/all_gather | solution.py:203
  10.7 146.0 %all-gather.17.cloned.1.call-start = ((), (), s32[]{:S(2)}) async-start(), calls=%async_computation.13 | async-start | bytes 5013504 | tf_op jit(solution)/shard_map/all_gather | solution.py:206
  12.6 226.8 %all-gather.15.cloned.1.call-start = ((), (), s32[]{:S(2)}) async-start(), calls=%async_computation.12 | async-start | bytes 10027008 | tf_op jit(solution)/shard_map/all_gather | solution.py:205
  13.5 732.1 %reduce-scatter.21.cloned.1.call-start = ((), (), s32[]{:S(2)}) async-start(), calls=%async_computation.15 | async-start | bytes 417792
  288.3 15.4 %copy-start = (f32[2,256,6144]{2,1,0:T(8,128)}, f32[2,256,6144]{2,1,0:T(8,128)S(1)}, u32[]{:S(2)}) copy-start(f32[2,256,6144]{2,1,0:T(8,128)S(1)} %get-tuple-element.1953) | copy-start | bytes 37748740 | tf_op jit(solution)/shard_map/while
  288.3 15.7 %copy-start.38 = (f32[768]{0:T(1024)S(1)}, f32[768]{0:T(1024)}, u32[]{:S(2)}) copy-start(f32[768]{0:T(1024)} %get-tuple-element.1805) | copy-start | bytes 9220 | tf_op jit(solution)/shard_map/while
  288.3 15.7 %copy-start.39 = (f32[768]{0:T(1024)S(1)}, f32[768]{0:T(1024)}, u32[]{:S(2)}) copy-start(f32[768]{0:T(1024)} %get-tuple-element.1806) | copy-start | bytes 9220 | tf_op jit(solution)/shard_map/while
  288.3 21.2 %copy-start.26 = (bf16[2,256,768]{2,1,0:T(8,128)(2,1)S(1)}, bf16[2,256,768]{2,1,0:T(8,128)(2,1)}, u32[]{:S(2)}) copy-start(bf16[2,256,768]{2,1,0:T(8,128)(2,1)} %get-tuple-element.1917) | copy-start | bytes 2359300 | tf_op jit(solution)/shard_map/while
  288.3 21.3 %copy-start.20 = (bf16[2,256,768]{2,1,0:T(8,128)(2,1)S(1)}, bf16[2,256,768]{2,1,0:T(8,128)(2,1)}, u32[]{:S(2)}) copy-start(bf16[2,256,768]{2,1,0:T(8,128)(2,1)} %get-tuple-element.1923) | copy-start | bytes 2359300 | tf_op jit(solution)/shard_map/while
  305.1 12.7 collective-permute-start
  348.9 15.4 %copy-start = (f32[2,256,6144]{2,1,0:T(8,128)}, f32[2,256,6144]{2,1,0:T(8,128)S(1)}, u32[]{:S(2)}) copy-start(f32[2,256,6144]{2,1,0:T(8,128)S(1)} %get-tuple-element.1953) | copy-start | bytes 37748740 | tf_op jit(solution)/shard_map/while
  348.9 15.7 %copy-start.38 = (f32[768]{0:T(1024)S(1)}, f32[768]{0:T(1024)}, u32[]{:S(2)}) copy-start(f32[768]{0:T(1024)} %get-tuple-element.1805) | copy-start | bytes 9220 | tf_op jit(solution)/shard_map/while
  348.9 15.7 %copy-start.39 = (f32[768]{0:T(1024)S(1)}, f32[768]{0:T(1024)}, u32[]{:S(2)}) copy-start(f32[768]{0:T(1024)} %get-tuple-element.1806) | copy-start | bytes 9220 | tf_op jit(solution)/shard_map/while
  348.9 22.2 %copy-start.26 = (bf16[2,256,768]{2,1,0:T(8,128)(2,1)S(1)}, bf16[2,256,768]{2,1,0:T(8,128)(2,1)}, u32[]{:S(2)}) copy-start(bf16[2,256,768]{2,1,0:T(8,128)(2,1)} %get-tuple-element.1917) | copy-start | bytes 2359300 | tf_op jit(solution)/shard_map/while
  348.9 22.2 %copy-start.20 = (bf16[2,256,768]{2,1,0:T(8,128)(2,1)S(1)}, bf16[2,256,768]{2,1,0:T(8,128)(2,1)}, u32[]{:S(2)}) copy-start(bf16[2,256,768]{2,1,0:T(8,128)(2,1)} %get-tuple-element.1923) | copy-start | bytes 2359300 | tf_op jit(solution)/shard_map/while
  365.7 13.0 %collective-permute-start = (bf16[256,768]{1,0:T(8,128)(2,1)}, bf16[256,768]{1,0:T(8,128)(2,1)}, u32[]{:S(2)}, u32[]{:S(2)}) collective-permute-start(bf16[256,768]{1,0:T(8,128)(2,1)} %get-tuple-element.1820), channel_id=1, source_target_pairs={{0,16},{1,17},{2,18},{3,19},{4,20},{5,21},{6,22},{7,23},{8,24},{9,... | collective-permute-start | bytes 1179656 | tf_op jit(solution)/shard_map/while/body/eval_jaxpr/ppermute | solution.py:17
  409.7 15.4 %copy-start = (f32[2,256,6144]{2,1,0:T(8,128)}, f32[2,256,6144]{2,1,0:T(8,128)S(1)}, u32[]{:S(2)}) copy-start(f32[2,256,6144]{2,1,0:T(8,128)S(1)} %get-tuple-element.1953) | copy-start | bytes 37748740 | tf_op jit(solution)/shard_map/while
  409.7 15.7 %copy-start.38 = (f32[768]{0:T(1024)S(1)}, f32[768]{0:T(1024)}, u32[]{:S(2)}) copy-start(f32[768]{0:T(1024)} %get-tuple-element.1805) | copy-start | bytes 9220 | tf_op jit(solution)/shard_map/while
  409.7 15.7 %copy-start.39 = (f32[768]{0:T(1024)S(1)}, f32[768]{0:T(1024)}, u32[]{:S(2)}) copy-start(f32[768]{0:T(1024)} %get-tuple-element.1806) | copy-start | bytes 9220 | tf_op jit(solution)/shard_map/while
  409.8 22.1 %copy-start.26 = (bf16[2,256,768]{2,1,0:T(8,128)(2,1)S(1)}, bf16[2,256,768]{2,1,0:T(8,128)(2,1)}, u32[]{:S(2)}) copy-start(bf16[2,256,768]{2,1,0:T(8,128)(2,1)} %get-tuple-element.1917) | copy-start | bytes 2359300 | tf_op jit(solution)/shard_map/while
  409.8 22.1 %copy-start.20 = (bf16[2,256,768]{2,1,0:T(8,128)(2,1)S(1)}, bf16[2,256,768]{2,1,0:T(8,128)(2,1)}, u32[]{:S(2)}) copy-start(bf16[2,256,768]{2,1,0:T(8,128)(2,1)} %get-tuple-element.1923) | copy-start | bytes 2359300 | tf_op jit(solution)/shard_map/while
  426.6 12.9 %collective-permute-start = (bf16[256,768]{1,0:T(8,128)(2,1)}, bf16[256,768]{1,0:T(8,128)(2,1)}, u32[]{:S(2)}, u32[]{:S(2)}) collective-permute-start(bf16[256,768]{1,0:T(8,128)(2,1)} %get-tuple-element.1820), channel_id=1, source_target_pairs={{0,16},{1,17},{2,18},{3,19},{4,20},{5,21},{6,22},{7,23},{8,24},{9,... | collective-permute-start | bytes 1179656 | tf_op jit(solution)/shard_map/while/body/eval_jaxpr/ppermute | solution.py:17
  463.3 12.5 copy-start.1
  489.3 26.7 %collective-permute-start.1 = (bf16[256,768]{1,0:T(8,128)(2,1)}, bf16[256,768]{1,0:T(8,128)(2,1)}, u32[]{:S(2)}, u32[]{:S(2)}) collective-permute-start(bf16[256,768]{1,0:T(8,128)(2,1)} %get-tuple-element.1876), channel_id=1, source_target_pairs={{16,0},{17,1},{18,2},{19,3},{20,4},{21,5},{22,6},{23,7},{24,8},{25... | collective-permute-start | bytes 1179656 | tf_op jit(solution)/shard_map/while/body/eval_jaxpr/ppermute | solution.py:17
  563.3 38.0 %collective-permute-start.1 = (bf16[256,768]{1,0:T(8,128)(2,1)}, bf16[256,768]{1,0:T(8,128)(2,1)}, u32[]{:S(2)}, u32[]{:S(2)}) collective-permute-start(bf16[256,768]{1,0:T(8,128)(2,1)} %get-tuple-element.1876), channel_id=1, source_target_pairs={{16,0},{17,1},{18,2},{19,3},{20,4},{21,5},{22,6},{23,7},{24,8},{25... | collective-permute-start | bytes 1179656 | tf_op jit(solution)/shard_map/while/body/eval_jaxpr/ppermute | solution.py:17
  648.6 38.0 %collective-permute-start.1 = (bf16[256,768]{1,0:T(8,128)(2,1)}, bf16[256,768]{1,0:T(8,128)(2,1)}, u32[]{:S(2)}, u32[]{:S(2)}) collective-permute-start(bf16[256,768]{1,0:T(8,128)(2,1)} %get-tuple-element.1876), channel_id=1, source_target_pairs={{16,0},{17,1},{18,2},{19,3},{20,4},{21,5},{22,6},{23,7},{24,8},{25... | collective-permute-start | bytes 1179656 | tf_op jit(solution)/shard_map/while/body/eval_jaxpr/ppermute | solution.py:17
  688.3 115.7 %reduce-scatter.19.cloned.1.call-start = ((), (), s32[]{:S(2)}) async-start(), calls=%async_computation.14 | async-start | bytes 417792
  690.0 180.4 %reduce-scatter.13.cloned.1.call-start = ((), (), s32[]{:S(2)}) async-start(), calls=%async_computation.7 | async-start | bytes 2506752 | tf_op jit(solution)/shard_map/reduce_scatter | solution.py:302
  690.8 273.8 %reduce-scatter.11.cloned.1.call-start = ((), (), s32[]{:S(2)}) async-start(), calls=%async_computation.6 | async-start | bytes 7520256 | tf_op jit(solution)/shard_map/reduce_scatter | solution.py:301
  691.5 388.6 %reduce-scatter.17.cloned.1.call-start = ((), (), s32[]{:S(2)}) async-start(), calls=%async_computation.9 | async-start | bytes 10027008 | tf_op jit(solution)/shard_map/reduce_scatter | solution.py:307
  692.3 587.6 %reduce-scatter.15.cloned.1.call-start = ((), (), s32[]{:S(2)}) async-start(), calls=%async_computation.8 | async-start | bytes 20054016 | tf_op jit(solution)/shard_map/reduce_scatter | solution.py:306
  (180 other events, 892.0 us)
Sparse Core Ops, SparseCore 0:
  10.9 42.0 all-gather.12
  55.9 45.6 all-gather.10
  104.4 52.2 all-gather.16
  159.4 79.9 all-gather.14
  688.4 57.1 reduce-scatter.20
  749.4 54.5 reduce-scatter.18
  808.4 62.0 reduce-scatter.12
  875.5 88.9 reduce-scatter.10
  969.2 110.8 reduce-scatter.16
  1085.2 194.5 reduce-scatter.14
where the time goes:
time: 1290 us
  waiting for transfers between devices  768 us (60%)
  matrix products  244 us (19%)
  local copies, waits for them, and re-layouts  119 us (9%)
  other arithmetic  71.3 us (6%)
  blocking collectives  43 us (3%)
  starting transfers between devices  19.6 us (2%)
  between operations  14.3 us (1%)
    reduce_scatter x1, waiting for transfers between devices, shards(): lax.psum_scatter(summed[2], 'dp', scatter_dimension=0, tiled=True)  200 us
    reduce_scatter x1, waiting for transfers between devices, shards(): lax.psum_scatter(summed[3], 'dp', scatter_dimension=0, tiled=True)  116 us
    unnamed x12, waiting for transfers between devices  112 us
    reduce_scatter x1, waiting for transfers between devices, shards(): lax.psum_scatter(summed[0], 'dp', scatter_dimension=0, tiled=True)  94.1 us
    all_gather x1, waiting for transfers between devices, shards(): lax.all_gather(w_gate_up[0].astype(jnp.bfloat16), 'dp', axis=0, tiled=True)  82.7 us
    reduce_scatter x1, waiting for transfers between devices, shards(): lax.psum_scatter(summed[1], 'dp', scatter_dimension=0, tiled=True)  65 us
    all_gather x1, waiting for transfers between devices, shards(): lax.all_gather(w_down[0].astype(jnp.bfloat16), 'dp', axis=0, tiled=True)  55.1 us
    dot_general x3, matrix products, layer_forward(): jnp.dot(gated_rows, down_matrix, preferred_element_type=jnp.float32)  46.1 us
  transfers between devices with their start and end apart: 16, of which 10 were waited for; matrix products, arithmetic and copies ran while one was open for 9% of the time, Pallas kernels for 0%

commit v1 on v0

--- a/solution.py
+++ b/solution.py
@@ -9,6 +9,18 @@
 FF = 3072
 EPSILON = 1e-05
 NEGATIVE = -1e30
+
+
+def gather_by_bits(x, axis, dim):
+    ways, here = (lax.axis_size(axis), lax.axis_index(axis))
+    grown, reach = (x, 1)
+    while reach < ways:
+        theirs = lax.ppermute(grown, axis, [(d, d ^ reach) for d in range(ways)])
+        mine_first = jnp.concatenate([grown, theirs], axis=dim)
+        theirs_first = jnp.concatenate([theirs, grown], axis=dim)
+        grown = jnp.where(here & reach == 0, mine_first, theirs_first)
+        reach = 2 * reach
+    return grown
 
 
 def shifted(shard, axis, by):
@@ -202,7 +214,7 @@
     forward_weights = (
         lax.all_gather(w_qkv[0].astype(jnp.bfloat16), "dp", axis=0, tiled=True),
         lax.all_gather(w_out[0].astype(jnp.bfloat16), "dp", axis=0, tiled=True),
-        lax.all_gather(w_gate_up[0].astype(jnp.bfloat16), "dp", axis=0, tiled=True),
+        gather_by_bits(w_gate_up[0].astype(jnp.bfloat16), "dp", 0),
         lax.all_gather(w_down[0].astype(jnp.bfloat16), "dp", axis=0, tiled=True),
         lax.all_gather(norm_gain[0].astype(jnp.bfloat16), "dp", axis=1, tiled=True),
         lax.all_gather(norm_bias[0].astype(jnp.bfloat16), "dp", axis=1, tiled=True),

time: 1290 us -> 1460 us (1.13)
  blocking collectives: 43 us -> 264 us
  waiting for transfers between devices: 768 us -> 690 us
  other arithmetic: 71.3 us -> 94.7 us
    all_gather x1, blocking collectives: 18.7 us -> 143 us  [shards(): lax.all_gather(norm_bias[0].astype(jnp.bfloat16), 'dp', axis=1, tiled=True)]
    ppermute x0 -> x4, waiting for transfers between devices: none -> 104 us  [gather_by_bits(): theirs = lax.ppermute(grown, axis, [(d, d ^ reach) for d in range(ways)])]
    all_gather x1, blocking collectives: 24.4 us -> 121 us  [shards(): lax.all_gather(norm_gain[0].astype(jnp.bfloat16), 'dp', axis=1, tiled=True)]
    all_gather x1, waiting for transfers between devices: 82.7 us -> 0.01 us  [shards(): lax.all_gather(w_gate_up[0].astype(jnp.bfloat16), 'dp', axis=0, tiled=True)]
    all_gather x1, waiting for transfers between devices: 55.1 us -> 0.01 us  [shards(): lax.all_gather(w_down[0].astype(jnp.bfloat16), 'dp', axis=0, tiled=True)]
    all_gather x1, waiting for transfers between devices: 42.9 us -> 0.01 us  [shards(): lax.all_gather(w_qkv[0].astype(jnp.bfloat16), 'dp', axis=0, tiled=True)]
    select_n x0 -> x4, other arithmetic: none -> 20.8 us  [gather_by_bits(): grown = jnp.where(here & reach == 0, mine_first, theirs_first)]
    dot_general x3, matrix products: 10.2 us -> 26 us  [layer_backward(): jnp.einsum('tf,df->td', gate_up_grad, gate_matrix, preferred_element_type...]
  transfers between devices with their start and end apart: 16 -> 20, of which waited for: 10 -> 9; matrix products, arithmetic and copies ran while one was open for 9% -> 20% of each run, Pallas kernels for 0% -> 0%
where the time goes in v1:
time: 1460 us
  waiting for transfers between devices  690 us (47%)
  blocking collectives  264 us (18%)
  matrix products  240 us (16%)
  local copies, waits for them, and re-layouts  126 us (9%)
  other arithmetic  94.7 us (6%)
  starting transfers between devices  23.8 us (2%)
    reduce_scatter x1, waiting for transfers between devices, shards(): lax.psum_scatter(summed[2], 'dp', scatter_dimension=0, tiled=True)  200 us
    all_gather x1, blocking collectives, shards(): lax.all_gather(norm_bias[0].astype(jnp.bfloat16), 'dp', axis=1, tiled=True)  143 us
    all_gather x1, blocking collectives, shards(): lax.all_gather(norm_gain[0].astype(jnp.bfloat16), 'dp', axis=1, tiled=True)  121 us
    reduce_scatter x1, waiting for transfers between devices, shards(): lax.psum_scatter(summed[3], 'dp', scatter_dimension=0, tiled=True)  116 us
    unnamed x12, waiting for transfers between devices  112 us
    ppermute x4, waiting for transfers between devices, gather_by_bits(): theirs = lax.ppermute(grown, axis, [(d, d ^ reach) for d in range(ways)])  104 us
    reduce_scatter x1, waiting for transfers between devices, shards(): lax.psum_scatter(summed[0], 'dp', scatter_dimension=0, tiled=True)  94.2 us
    reduce_scatter x1, waiting for transfers between devices, shards(): lax.psum_scatter(summed[1], 'dp', scatter_dimension=0, tiled=True)  65 us
  transfers between devices with their start and end apart: 20, of which 9 were waited for; matrix products, arithmetic and copies ran while one was open for 20% of the time, Pallas kernels for 0%

profile of v1, /device:TPU:0, one launch (start us, length us, event | category | flops | bytes accessed | tf_op | source)
XLA Modules:
  0.0 1459.1 jit_solution(3446551039515062742)
XLA Ops:
  18.2 29.5 %collective-permute-done.3 = bf16[96,6144]{1,0:T(8,128)(2,1)} collective-permute-done((bf16[96,6144]{1,0:T(8,128)(2,1)S(1)}, bf16[96,6144]{1,0:T(8,128)(2,1)}, u32[]{:S(2)}, u32[]{:S(2)}) %collective-permute-start.3) | collective-permute-done | bytes 1179680 | tf_op jit(solution)/shard_map/ppermute | solution.py:18
  51.7 72.6 %collective-permute-done.4 = bf16[192,6144]{1,0:T(8,128)(2,1)} collective-permute-done((bf16[192,6144]{1,0:T(8,128)(2,1)S(1)}, bf16[192,6144]{1,0:T(8,128)(2,1)}, u32[]{:S(2)}, u32[]{:S(2)}) %collective-permute-start.4) | collective-permute-done | bytes 2359328 | tf_op jit(solution)/shard_map/ppermute | solution.py:18
  124.3 6.4 maximum_select_fusion.1
  134.3 120.8 %all-gather.2 = bf16[1,2,768]{1,0,2:T(2,128)(2,1)S(1)} all-gather(bf16[1,2,48]{1,0,2:T(2,128)(2,1)S(1)} %copy.83), channel_id=4, replica_groups=mesh['section'=2,'dp'=16] {'dp'}, dimensions={2}, use_global_device_ids=true | all-gather | bytes 3264 | tf_op jit(solution)/shard_map/all_gather | solution.py:219
  255.9 142.9 %all-gather.3 = bf16[1,2,768]{1,0,2:T(2,128)(2,1)S(1)} all-gather(bf16[1,2,48]{1,0,2:T(2,128)(2,1)S(1)} %copy.85), channel_id=5, replica_groups=mesh['section'=2,'dp'=16] {'dp'}, dimensions={2}, use_global_device_ids=true | all-gather | bytes 3264 | tf_op jit(solution)/shard_map/all_gather | solution.py:220
  399.7 12.1 maximum_select_fusion
  429.6 169.1 %while.65 = (s32[]{:T(128)}, bf16[256,768]{1,0:T(8,128)(2,1)}, bf16[2,256,768]{2,1,0:T(8,128)(2,1)}, bf16[2,256,768]{2,1,0:T(8,128)(2,1)}, bf16[2,256,1536]{2,1,...) while((s32[]{:T(128)}, bf16[256,768]{1,0:T(8,128)(2,1)}, ...), condition=%wide.region_7.8_spmd, body=%wide.region_0.7_spmd.sunk | while | flops 5104144384 | bytes 180324528 | solution.py:265
  460.0 11.2 fusion.202
  510.3 6.3 bitcast_dynamic-update-slice_fusion.15
  516.6 11.2 fusion.202
  573.0 11.2 fusion.202
  601.2 258.6 %while.66 = (s32[]{:T(128)}, bf16[256,768]{1,0:T(8,128)(2,1)}, f32[768,2304]{1,0:T(8,128)}, f32[768,768]{1,0:T(8,128)}, f32[768,6144]{1,0:T(8,128)}, /*index=5*/...) while((s32[]{:T(128)}, bf16[256,768]{1,0:T(8,128)(2,1)}, ...), condition=%wide.region_18.19_spmd.clone, body=%wide.region_8.18_spmd.clone.sunk | while | flops 10294599680 | bytes 311429440 | solution.py:309
  624.0 10.6 multiply_convert_fusion.8
  634.7 8.7 fusion.227
  656.7 7.2 select_add_fusion.11
  669.1 8.4 select_add_fusion.10
  703.3 10.6 multiply_convert_fusion.8
  714.0 8.7 fusion.227
  737.0 10.0 select_add_fusion.11
  747.0 7.3 select_add_fusion.8
  754.3 12.0 select_add_fusion.10
  793.0 10.6 multiply_convert_fusion.8
  803.7 8.7 fusion.227
  826.8 10.0 select_add_fusion.11
  836.7 7.3 select_add_fusion.8
  844.0 12.0 select_add_fusion.10
  866.0 52.1 %reduce-scatter.21.cloned.1.call-done = f32[48,2]{1,0:T(8,128)} async-done(((f32[768,2]{1,0:T(8,128)}), f32[48,2]{1,0:T(8,128)}) %reduce-scatter.21.cloned.1.call-update) | async-done | bytes 400
  919.5 57.0 %reduce-scatter.19.cloned.1.call-done = f32[48,2]{1,0:T(8,128)} async-done(((f32[768,2]{1,0:T(8,128)}), f32[48,2]{1,0:T(8,128)}) %reduce-scatter.19.cloned.1.call-update) | async-done | bytes 400
  977.9 65.0 %reduce-scatter.13.cloned.1.call-done = f32[48,768]{1,0:T(8,128)} async-done(((f32[768,768]{1,0:T(8,128)}), f32[48,768]{1,0:T(8,128)}) %reduce-scatter.13.cloned.1.call-update) | async-done | bytes 147472 | tf_op jit(solution)/shard_map/reduce_scatter | solution.py:314
  1042.8 94.2 %reduce-scatter.11.cloned.1.call-done = f32[48,2304]{1,0:T(8,128)} async-done(((f32[768,2304]{1,0:T(8,128)}), f32[48,2304]{1,0:T(8,128)}) %reduce-scatter.11.cloned.1.call-update) | async-done | bytes 442384 | tf_op jit(solution)/shard_map/reduce_scatter | solution.py:313
  1137.0 115.6 %reduce-scatter.17.cloned.1.call-done = f32[192,768]{1,0:T(8,128)} async-done(((f32[3072,768]{1,0:T(8,128)}), f32[192,768]{1,0:T(8,128)}) %reduce-scatter.17.cloned.1.call-update) | async-done | bytes 589840 | tf_op jit(solution)/shard_map/reduce_scatter | solution.py:319
  1252.6 199.6 %reduce-scatter.15.cloned.1.call-done = f32[48,6144]{1,0:T(8,128)} async-done(((f32[768,6144]{1,0:T(8,128)}), f32[48,6144]{1,0:T(8,128)}) %reduce-scatter.15.cloned.1.call-update) | async-done | bytes 1179664 | tf_op jit(solution)/shard_map/reduce_scatter | solution.py:318
  (686 shorter events, 298.5 us)
Async XLA Ops:
  7.2 404.6 %all-gather.13.cloned.1.call-start = ((), (), s32[]{:S(2)}) async-start(), calls=%async_computation.11 | async-start | bytes 1253376 | tf_op jit(solution)/shard_map/all_gather | solution.py:216
  8.9 402.9 %all-gather.11.cloned.1.call-start = ((), (), s32[]{:S(2)}) async-start(), calls=%async_computation.10 | async-start | bytes 3760128 | tf_op jit(solution)/shard_map/all_gather | solution.py:215
  10.7 401.1 %all-gather.15.cloned.1.call-start = ((), (), s32[]{:S(2)}) async-start(), calls=%async_computation.12 | async-start | bytes 5013504 | tf_op jit(solution)/shard_map/all_gather | solution.py:218
  12.0 2.1 collective-permute-start.2
  14.4 33.3 %collective-permute-start.3 = (bf16[96,6144]{1,0:T(8,128)(2,1)S(1)}, bf16[96,6144]{1,0:T(8,128)(2,1)}, u32[]{:S(2)}, u32[]{:S(2)}) collective-permute-start(bf16[96,6144]{1,0:T(8,128)(2,1)S(1)} %maximum_select_fusion.3), channel_id=1, source_target_pairs={{0,2},{1,3},{2,0},{3,1},{4,6},{5,7},{6,4},{7,5},{8,10},{9,11},{10,... | collective-permute-start | bytes 3538952 | tf_op jit(solution)/shard_map/ppermute | solution.py:18
  18.1 580.5 %all-gather.17.cloned.1.call-start = ((), (), s32[]{:S(2)}) async-start(), calls=%async_computation.13 | async-start | bytes 10027008 | tf_op jit(solution)/shard_map/all_gather | solution.py:269
  49.8 74.5 %collective-permute-start.4 = (bf16[192,6144]{1,0:T(8,128)(2,1)S(1)}, bf16[192,6144]{1,0:T(8,128)(2,1)}, u32[]{:S(2)}, u32[]{:S(2)}) collective-permute-start(bf16[192,6144]{1,0:T(8,128)(2,1)S(1)} %maximum_select_fusion.2), channel_id=1, source_target_pairs={{0,4},{1,5},{2,6},{3,7},{4,0},{5,1},{6,2},{7,3},{8,12},{9,13},{10,... | collective-permute-start | bytes 7077896 | tf_op jit(solution)/shard_map/ppermute | solution.py:18
  51.7 81.3 %copy-start.26 = (f32[1,48,6144]{2,1,0:T(8,128)S(1)}, f32[1,48,6144]{2,1,0:T(8,128)}, u32[]{:S(2)}) copy-start(f32[1,48,6144]{2,1,0:T(8,128)} %param.17) | copy-start | bytes 3538948
  51.7 82.3 %copy-start.56 = (f32[1,2,48]{2,1,0:T(2,128)S(1)}, f32[1,2,48]{2,1,0:T(2,128)}, u32[]{:S(2)}) copy-start(f32[1,2,48]{2,1,0:T(2,128)} %param.19) | copy-start | bytes 1156
  51.7 82.3 %copy-start.57 = (f32[1,2,48]{2,1,0:T(2,128)S(1)}, f32[1,2,48]{2,1,0:T(2,128)}, u32[]{:S(2)}) copy-start(f32[1,2,48]{2,1,0:T(2,128)} %param.20) | copy-start | bytes 1156
  130.7 269.0 %collective-permute-start.5 = (bf16[384,6144]{1,0:T(8,128)(2,1)}, bf16[384,6144]{1,0:T(8,128)(2,1)}, u32[]{:S(2)}, u32[]{:S(2)}) collective-permute-start(bf16[384,6144]{1,0:T(8,128)(2,1)} %maximum_select_fusion.1), channel_id=1, source_target_pairs={{0,8},{1,9},{2,10},{3,11},{4,12},{5,13},{6,14},{7,15},{8,0},{9,1},... | collective-permute-start | bytes 14155784 | tf_op jit(solution)/shard_map/ppermute | solution.py:18
  133.9 784.2 %reduce-scatter.21.cloned.1.call-start = ((), (), s32[]{:S(2)}) async-start(), calls=%async_computation.15 | async-start | bytes 417792
  460.0 16.8 %copy-start.22 = (bf16[2,256,768]{2,1,0:T(8,128)(2,1)S(1)}, bf16[2,256,768]{2,1,0:T(8,128)(2,1)}, u32[]{:S(2)}) copy-start(bf16[2,256,768]{2,1,0:T(8,128)(2,1)} %get-tuple-element.1917) | copy-start | bytes 2359300 | tf_op jit(solution)/shard_map/while
  460.0 16.9 %copy-start.19 = (bf16[2,256,768]{2,1,0:T(8,128)(2,1)S(1)}, bf16[2,256,768]{2,1,0:T(8,128)(2,1)}, u32[]{:S(2)}) copy-start(bf16[2,256,768]{2,1,0:T(8,128)(2,1)} %get-tuple-element.1923) | copy-start | bytes 2359300 | tf_op jit(solution)/shard_map/while
  472.6 13.7 collective-permute-start
  516.6 16.7 %copy-start.22 = (bf16[2,256,768]{2,1,0:T(8,128)(2,1)S(1)}, bf16[2,256,768]{2,1,0:T(8,128)(2,1)}, u32[]{:S(2)}) copy-start(bf16[2,256,768]{2,1,0:T(8,128)(2,1)} %get-tuple-element.1917) | copy-start | bytes 2359300 | tf_op jit(solution)/shard_map/while
  516.6 16.7 %copy-start.19 = (bf16[2,256,768]{2,1,0:T(8,128)(2,1)S(1)}, bf16[2,256,768]{2,1,0:T(8,128)(2,1)}, u32[]{:S(2)}) copy-start(bf16[2,256,768]{2,1,0:T(8,128)(2,1)} %get-tuple-element.1923) | copy-start | bytes 2359300 | tf_op jit(solution)/shard_map/while
  529.2 13.6 collective-permute-start
  573.0 16.0 %copy-start.22 = (bf16[2,256,768]{2,1,0:T(8,128)(2,1)S(1)}, bf16[2,256,768]{2,1,0:T(8,128)(2,1)}, u32[]{:S(2)}) copy-start(bf16[2,256,768]{2,1,0:T(8,128)(2,1)} %get-tuple-element.1917) | copy-start | bytes 2359300 | tf_op jit(solution)/shard_map/while
  573.0 16.1 %copy-start.19 = (bf16[2,256,768]{2,1,0:T(8,128)(2,1)S(1)}, bf16[2,256,768]{2,1,0:T(8,128)(2,1)}, u32[]{:S(2)}) copy-start(bf16[2,256,768]{2,1,0:T(8,128)(2,1)} %get-tuple-element.1923) | copy-start | bytes 2359300 | tf_op jit(solution)/shard_map/while
  585.7 12.9 collective-permute-start
  622.4 12.3 copy-start
  652.8 27.6 %collective-permute-start.1 = (bf16[256,768]{1,0:T(8,128)(2,1)}, bf16[256,768]{1,0:T(8,128)(2,1)}, u32[]{:S(2)}, u32[]{:S(2)}) collective-permute-start(bf16[256,768]{1,0:T(8,128)(2,1)} %get-tuple-element.1876), channel_id=1, source_target_pairs={{16,0},{17,1},{18,2},{19,3},{20,4},{21,5},{22,6},{23,7},{24,8},{25... | collective-permute-start | bytes 1179656 | tf_op jit(solution)/shard_map/while/body/eval_jaxpr/ppermute | solution.py:29
  701.6 12.3 copy-start
  732.0 38.0 %collective-permute-start.1 = (bf16[256,768]{1,0:T(8,128)(2,1)}, bf16[256,768]{1,0:T(8,128)(2,1)}, u32[]{:S(2)}, u32[]{:S(2)}) collective-permute-start(bf16[256,768]{1,0:T(8,128)(2,1)} %get-tuple-element.1876), channel_id=1, source_target_pairs={{16,0},{17,1},{18,2},{19,3},{20,4},{21,5},{22,6},{23,7},{24,8},{25... | collective-permute-start | bytes 1179656 | tf_op jit(solution)/shard_map/while/body/eval_jaxpr/ppermute | solution.py:29
  791.3 12.3 copy-start
  821.7 38.1 %collective-permute-start.1 = (bf16[256,768]{1,0:T(8,128)(2,1)}, bf16[256,768]{1,0:T(8,128)(2,1)}, u32[]{:S(2)}, u32[]{:S(2)}) collective-permute-start(bf16[256,768]{1,0:T(8,128)(2,1)} %get-tuple-element.1876), channel_id=1, source_target_pairs={{16,0},{17,1},{18,2},{19,3},{20,4},{21,5},{22,6},{23,7},{24,8},{25... | collective-permute-start | bytes 1179656 | tf_op jit(solution)/shard_map/while/body/eval_jaxpr/ppermute | solution.py:29
  861.5 115.0 %reduce-scatter.19.cloned.1.call-start = ((), (), s32[]{:S(2)}) async-start(), calls=%async_computation.14 | async-start | bytes 417792
  863.2 179.7 %reduce-scatter.13.cloned.1.call-start = ((), (), s32[]{:S(2)}) async-start(), calls=%async_computation.7 | async-start | bytes 2506752 | tf_op jit(solution)/shard_map/reduce_scatter | solution.py:314
  863.9 273.1 %reduce-scatter.11.cloned.1.call-start = ((), (), s32[]{:S(2)}) async-start(), calls=%async_computation.6 | async-start | bytes 7520256 | tf_op jit(solution)/shard_map/reduce_scatter | solution.py:313
  864.7 387.9 %reduce-scatter.17.cloned.1.call-start = ((), (), s32[]{:S(2)}) async-start(), calls=%async_computation.9 | async-start | bytes 10027008 | tf_op jit(solution)/shard_map/reduce_scatter | solution.py:319
  865.4 586.8 %reduce-scatter.15.cloned.1.call-start = ((), (), s32[]{:S(2)}) async-start(), calls=%async_computation.8 | async-start | bytes 20054016 | tf_op jit(solution)/shard_map/reduce_scatter | solution.py:318
  (167 other events, 870.4 us)
Sparse Core Ops, SparseCore 0:
  10.9 43.8 all-gather.12
  57.6 58.2 all-gather.10
  118.7 169.3 all-gather.14
  290.8 160.7 all-gather.16
  861.6 56.4 reduce-scatter.20
  921.9 54.5 reduce-scatter.18
  980.8 61.9 reduce-scatter.12
  1048.0 89.0 reduce-scatter.10
  1141.7 110.8 reduce-scatter.16
  1257.7 194.5 reduce-scatter.14
